TPU v7x, 32 devices: a whole 2x2x4 slice. The times are simulated.
32 devices in a mesh: space: 8 (over z, x), taxa: 4 (over y, core).
Axes of the slice: x: 2, y: 2, z: 4, core: 2. Of those that a mesh axis runs over, the one named last changes fastest.
Arguments:
- biomass: float32 [2048, 64, 256], P('taxa', 'space'), may hold values from 0.1 to 2
- enzymes: float32 [40, 64, 256], P(None, 'space'), may hold values from 0.1 to 1
- substrates: float32 [12, 64, 256], P(None, 'space'), may hold values from 0.5 to 5
- monomers: float32 [14, 64, 256], P(None, 'space'), may hold values from 0.1 to 2
- enz_traits: int32 [2048, 40], P('taxa'), may hold values 0 or 1
- mono_traits: int32 [2048, 14], P('taxa'), may hold values 0 or 1
- enz_target: int32 [40], replicated, may hold values from 0 to 11
- prod_rate: float32 [2048], P('taxa'), may hold values from 0.002 to 0.02
- uptake_rate: float32 [2048], P('taxa'), may hold values from 0.0005 to 0.005
- mortality: float32 [2048], P('taxa'), may hold values from 0.02 to 0.1
- disperse: float32 [2048], P('taxa'), may hold values from 0.1 to 0.5
- enz_loss: float32 [40], replicated, may hold values from 0.05 to 0.3
- vmax: float32 [40], replicated, may hold values from 0.05 to 0.5
- kmich: float32 [40], replicated, may hold values from 0.5 to 5
- khalf: float32 [14], replicated, may hold values from 0.5 to 5
- offsets: int32 [8, 2], replicated, may hold values from -2 to 2, as said below
Outputs:
- biomass_out: float32 [2048, 64, 256], P('taxa', 'space')
- enzymes_out: float32 [40, 64, 256], P(None, 'space')
- substrates_out: float32 [12, 64, 256], P(None, 'space')
- monomers_out: float32 [14, 64, 256], P(None, 'space')
Inputs may be any that keep to these rules, and one draw needn't show every extreme that they name: Offsets lie in -2 to 2 in both entries and are never both zero; among the row offsets, -2 and 2 each appear twice.
All inputs are finite; a program needn't handle non-finite values. No bound on the sum of `enz_traits` or of `mono_traits` on one device may be relied on, other than what follows from the above.
Results may differ from a plain program's by a relative error of at most 0.00011.
Values sent between devices are 32-bit elements; how exact they have to be, the bound alone decides.
No kernel may reach another device: no remote copies, remote signals or barrier semaphores. Data moves between devices by JAX's collectives and lax.ppermute only.
A program may use at most 128 MiB of HBM per device.

v0:
```python
import jax
import jax.numpy as jnp
from jax import lax
from jax.sharding import PartitionSpec as P

KOFF = 8
DAYS = 2
HIGH = lax.Precision.HIGHEST
YIELD = 0.6


def extended(block, sides, width):
    for axis, dim in sides:
        count = lax.axis_size(axis)
        forward = [(i, i + 1) for i in range(count - 1)]
        forward.append((count - 1, 0))
        backward = [(target, source) for source, target in forward]
        low = lax.ppermute(
            lax.slice_in_dim(block, block.shape[dim] - width, None, axis=dim), axis, forward
        )
        high = lax.ppermute(lax.slice_in_dim(block, 0, width, axis=dim), axis, backward)
        block = jnp.concatenate([low, block, high], axis=dim)
    return block


def cell_update(sums, enz, sub, mono, enz_loss, vmax, kmich, khalf, enz_target):
    n_enz = enz.shape[0]
    made = sums[:n_enz]
    demand = sums[n_enz:]
    pool = enz * (1.0 - enz_loss)[:, None, None] + made
    pick = (enz_target[:, None] == lax.iota(jnp.int32, sub.shape[0])[None, :]).astype(jnp.float32)
    target_sub = jnp.einsum("es,srw->erw", pick, sub, precision=HIGH)
    speed = vmax[:, None, None] * pool / (kmich[:, None, None] + target_sub)
    rate = jnp.einsum("es,erw->srw", pick, speed, precision=HIGH)
    left = sub * jnp.exp(-rate)
    freed = sub - left
    extra = jnp.zeros((mono.shape[0] - sub.shape[0],) + sub.shape[1:], jnp.float32)
    mono_one = mono + jnp.concatenate([freed, extra], 0)
    share = mono_one / (khalf[:, None, None] + demand + mono_one)
    mono_two = mono_one - demand * share
    return (pool, left, mono_two, share)


def pool_update(bio, enz, sub, mono, prod_w, upt_w, enz_loss, vmax, kmich, khalf, enz_target):
    count, rows, width = bio.shape
    flat = bio.reshape(count, rows * width)
    made = jnp.dot(prod_w.T, flat, precision=HIGH, preferred_element_type=jnp.float32)
    need = jnp.dot(upt_w.T, flat, precision=HIGH, preferred_element_type=jnp.float32)
    local = jnp.concatenate([made, need], 0).reshape(-1, rows, width)
    sums = lax.psum(local, "taxa")
    return cell_update(sums, enz, sub, mono, enz_loss, vmax, kmich, khalf, enz_target)


def grow(bio, share, mono_w, uptake_rate, keep):
    gain = jnp.einsum("tm,mrw->trw", mono_w, share, precision=HIGH)
    return bio * (keep[:, None, None] + YIELD * uptake_rate[:, None, None] * gain)


def spread(grown_pad, disperse, offsets, rows):
    fraction = disperse[:, None, None]
    moved_pad = grown_pad * fraction
    centre = grown_pad[:, 2 : 2 + rows]
    total = jnp.zeros_like(centre)
    for k in range(KOFF):
        piece = lax.dynamic_slice_in_dim(moved_pad, 2 - offsets[k, 0], rows, 1)
        total = total + jnp.roll(piece, offsets[k, 1], axis=2)
    return centre - centre * fraction + total / KOFF


def body(
    biomass,
    enzymes,
    substrates,
    monomers,
    enz_traits,
    mono_traits,
    enz_target,
    prod_rate,
    uptake_rate,
    mortality,
    disperse,
    enz_loss,
    vmax,
    kmich,
    khalf,
    offsets,
):
    prod_w = enz_traits.astype(jnp.float32) * prod_rate[:, None]
    mono_w = mono_traits.astype(jnp.float32)
    upt_w = mono_w * uptake_rate[:, None]
    keep = 1.0 - mortality - prod_rate * jnp.sum(enz_traits.astype(jnp.float32), axis=1)
    rows = biomass.shape[1]
    bio = biomass
    for day in range(DAYS):
        enzymes, substrates, monomers, share = pool_update(
            bio,
            enzymes,
            substrates,
            monomers,
            prod_w,
            upt_w,
            enz_loss,
            vmax,
            kmich,
            khalf,
            enz_target,
        )
        grown = grow(bio, share, mono_w, uptake_rate, keep)
        padded = extended(grown, (("space", 1),), 2)
        bio = spread(padded, disperse, offsets, rows)
    return (bio, enzymes, substrates, monomers)


def solution(mesh):
    placed = (
        P("taxa", "space", None),
        P(None, "space", None),
        P(None, "space", None),
        P(None, "space", None),
        P("taxa", None),
        P("taxa", None),
        P(),
        P("taxa"),
        P("taxa"),
        P("taxa"),
        P("taxa"),
        P(),
        P(),
        P(),
        P(),
        P(),
    )
    return jax.shard_map(
        body,
        mesh=mesh,
        in_specs=placed,
        out_specs=(
            P("taxa", "space", None),
            P(None, "space", None),
            P(None, "space", None),
            P(None, "space", None),
        ),
        check_vma=False,
    )
```

profile of v0, /device:TPU:0, one launch (start us, length us, event | category | flops | bytes accessed | tf_op | source)
XLA Modules:
  0.0 286.9 jit_solution(10821046505881652321)
XLA Ops:
  7.2 0.0 all-reduce.5.cloned.1.call-start
  7.2 4.2 %copy.41 = f32[64,8,8,256]{3,1,2,0:T(8,128)S(1)} copy(f32[64,8,8,256]{3,2,1,0:T(8,128)} %bitcast.63) | data formatting | bytes 8388608
  11.4 0.0 copy-start.4
  11.4 0.0 copy-start.14
  11.4 0.0 copy-done.6
  11.4 0.0 copy-done.13
  11.4 2.1 fusion.50
  13.5 2.5 fusion.42
  16.1 0.1 copy.42
  16.3 0.9 copy.31
  17.2 0.0 all-reduce.5.cloned.1.call-update
  17.2 0.0 all-reduce.7.cloned.1.call-start
  17.3 0.0 copy-start.17
  17.3 0.0 copy-start.18
  17.3 0.0 copy-start.8
  17.3 0.0 copy-start.10
  17.3 0.0 copy-start.16
  17.4 0.0 copy-start.19
  17.4 0.0 copy-start.20
  17.4 0.0 copy-start.5
  17.4 0.0 copy-start.15
  17.4 5.4 %copy.35 = f32[512,8,256]{0,2,1:T(8,128)} copy(f32[512,8,256]{2,1,0:T(8,128)} %param.18) | data formatting | bytes 8388608 | tf_op args[0]
  22.8 30.3 %all-reduce.5.cloned.1.call-done = f32[54,8,256]{2,0,1:T(8,128)} async-done(((f32[54,8,256]{2,0,1:T(8,128)}), f32[54,8,256]{2,0,1:T(8,128)}) %all-reduce.5.cloned.1.call-update) | async-done | bytes 442384 | tf_op jit(solution)/shard_map/psum | solution.py:50
  53.1 1.4 fusion.35
  54.5 0.9 copy_subtract_fusion
  55.4 7.1 %bitcast_multiply_fusion.1 = f32[512,8,256]{0,2,1:T(8,128)S(1)} fusion(f32[512,8,256]{0,2,1:T(8,128)} %copy.35, f32[512]{0:T(512)S(1)} %get-tuple-element.56, f32[512]{0:T(512)S(1)} %get-tuple-element.55, s32[512,14]{0,1:T(8,128)S(1)} %copy-done.6, f32[54,8,256]{2,0,1:T(8,128)} %all-reduce.5.cloned.1.call-done, f32[14]{0:T(128)S(1)} %copy-done.15, ...), kind=kOutput, calls=%fused_computation.71 | convolution fusion | flops 179428352 | bytes 8765496 | tf_op jit(solution)/shard_map/tm,mrw->trw/dot_general | solution.py:55
  62.5 0.0 copy-start.1
  62.5 2.0 copy-done.1
  64.5 0.2 fusion.63
  64.7 1.5 collective-permute-start
  66.2 3.2 %collective-permute-start.1 = (f32[512,2,256]{0,2,1:T(8,128)S(1)}, f32[512,2,256]{0,2,1:T(8,128)}, u32[]{:S(2)}, u32[]{:S(2)}) collective-permute-start(f32[512,2,256]{0,2,1:T(8,128)S(1)} %get-tuple-element.34), channel_id=1, source_target_pairs={{4,0},{8,4},{12,8},{16,12},{20,16},{24,20},{28,24},{0,28},{5,1},{9... | collective-permute-start | bytes 3145736 | tf_op jit(solution)/shard_map/ppermute | solution.py:21
  69.5 0.7 fusion.64
  95.8 14.2 %collective-permute-done = f32[512,2,256]{0,2,1:T(8,128)S(1)} collective-permute-done((f32[512,2,256]{0,2,1:T(8,128)S(1)}, f32[512,2,256]{0,2,1:T(8,128)S(1)}, u32[]{:S(2)}, u32[]{:S(2)}) %collective-permute-start) | collective-permute-done | bytes 1048608 | tf_op jit(solution)/shard_map/ppermute | solution.py:18
  110.0 2.3 collective-permute-done.1
  112.3 3.0 %maximum_multiply_fusion = f32[512,12,256]{0,2,1:T(8,128)S(1)} fusion(f32[512,2,256]{0,2,1:T(8,128)} %collective-permute-done.1, f32[512,8,256]{0,2,1:T(8,128)} %copy-done.1, f32[512,2,256]{0,2,1:T(8,128)S(1)} %collective-permute-done, f32[512]{0:T(512)S(1)} %copy-done.12), kind=kLoop, calls=%fused_computation.32 | loop fusion | flops 4718592 | bytes 12584960 | tf_op jit(solution)/shard_map/mul | solution.py:61
  115.3 12.3 %constant_dynamic-slice_fusion.15 = (f32[512,8,256]{0,2,1:T(8,128)}, f32[512,8,256]{0,2,1:T(8,128)}, f32[512,8,256]{0,2,1:T(8,128)}, f32[512,8,256]{0,2,1:T(8,12...) fusion(f32[512,12,256]{0,2,1:T(8,128)S(1)} %maximum_multiply_fusion, ...), kind=kLoop, calls=%fused_computation.124 | loop fusion | bytes 67108896 | tf_op jit(solution)/shard_map/dynamic_slice | solution.py:65
  127.6 16.5 %fusion = f32[512,8,256]{0,2,1:T(8,128)S(1)} fusion(f32[512,8,256]{0,2,1:T(8,128)} %copy-done.1, s32[]{:T(128)S(6)} %select_n.95, f32[512,8,256]{0,2,1:T(8,128)} %get-tuple-element.24, s32[]{:T(128)S(6)} %select_n.93, f32[512,8,256]{0,2,1:T(8,128)} %get-tuple-element.25, s32[]{:T(128)S(6)} %select_n.91, f32[512,8,256]{0,2,1:T(8,128)} %get-tuple-element.26, ...), kind=kLoop, calls=%fused_computation.36 | loop fusion | flops 19922944 | bytes 41945120 | tf_op jit(solution)/shard_map/add | solution.py:67
  144.1 0.0 copy-start
  144.1 3.5 %fusion.49 = f32[14,2048]{1,0:T(8,128)S(1)} fusion(f32[512,2048]{0,1:T(8,128)S(1)} %bitcast.59, s32[512,14]{0,1:T(8,128)S(1)} %copy-done.6, f32[512]{0:T(512)S(1)} %copy-done.13), kind=kOutput, calls=%fused_computation.105 | convolution fusion | flops 176175104 | bytes 4339712 | tf_op jit(solution)/shard_map/dot_general | solution.py:48
  147.7 0.0 copy-start.9
  147.7 0.0 copy-start.7
  147.7 4.0 %fusion.41 = f32[40,2048]{1,0:T(8,128)S(1)} fusion(f32[512,2048]{0,1:T(8,128)S(1)} %bitcast.60, s32[512,40]{0,1:T(8,128)S(1)} %copy-done.4, f32[512]{0:T(512)S(1)} %copy-done.14), kind=kOutput, calls=%fused_computation.96 | convolution fusion | flops 503357440 | bytes 4605952 | tf_op jit(solution)/shard_map/dot_general | solution.py:47
  151.8 0.1 copy.43
  151.9 0.9 copy.36
  152.9 0.0 all-reduce.7.cloned.1.call-update
  152.9 32.7 %all-reduce.7.cloned.1.call-done = f32[54,8,256]{2,0,1:T(8,128)} async-done(((f32[54,8,256]{2,0,1:T(8,128)}), f32[54,8,256]{2,0,1:T(8,128)}) %all-reduce.7.cloned.1.call-update) | async-done | bytes 442384 | tf_op jit(solution)/shard_map/psum | solution.py:50
  185.6 1.1 slice_add_fusion
  186.7 0.4 fusion.34
  187.1 0.2 fusion.65
  187.3 1.0 multiply_subtract_fusion.2
  188.4 7.2 %bitcast_multiply_fusion = f32[512,8,256]{0,2,1:T(8,128)S(1)} fusion(f32[512,8,256]{0,2,1:T(8,128)} %copy-done, f32[512]{0:T(512)S(1)} %get-tuple-element.56, f32[512]{0:T(512)S(1)} %get-tuple-element.55, s32[512,14]{0,1:T(8,128)S(1)} %copy-done.6, f32[14,8,256]{2,0,1:T(8,128)S(1)} %get-tuple-element.14, f32[54,8,256]{2,0,1:T(8,128)} %all-reduce.7.cloned.1.call-done, ...), kind=kOutput, calls=%fused_computation.70 | convolution fusion | flops 179399680 | bytes 8667192 | tf_op jit(solution)/shard_map/tm,mrw->trw/dot_general | solution.py:55
  195.5 0.0 copy-start.2
  195.6 0.2 fusion.62
  195.8 1.5 collective-permute-start.2
  197.3 3.3 %collective-permute-start.3 = (f32[512,2,256]{0,2,1:T(8,128)S(1)}, f32[512,2,256]{0,2,1:T(8,128)S(1)}, u32[]{:S(2)}, u32[]{:S(2)}) collective-permute-start(f32[512,2,256]{0,2,1:T(8,128)S(1)} %get-tuple-element.32), channel_id=1, source_target_pairs={{4,0},{8,4},{12,8},{16,12},{20,16},{24,20},{28,24},{0,28},{5,1},{9... | collective-permute-start | bytes 3145736 | tf_op jit(solution)/shard_map/ppermute | solution.py:21
  200.6 0.8 copy.38
  201.4 0.7 copy.40
  202.1 0.7 copy.39
  202.8 38.3 %collective-permute-done.2 = f32[512,2,256]{0,2,1:T(8,128)S(1)} collective-permute-done((f32[512,2,256]{0,2,1:T(8,128)S(1)}, f32[512,2,256]{0,2,1:T(8,128)S(1)}, u32[]{:S(2)}, u32[]{:S(2)}) %collective-permute-start.2) | collective-permute-done | bytes 1048608 | tf_op jit(solution)/shard_map/ppermute | solution.py:18
  241.1 2.2 collective-permute-done.3
  243.3 0.8 maximum_multiply_fusion.1
  244.1 12.3 %constant_dynamic-slice_fusion.7 = (f32[512,8,256]{0,2,1:T(8,128)}, f32[512,8,256]{0,2,1:T(8,128)}, f32[512,8,256]{0,2,1:T(8,128)}, f32[512,8,256]{0,2,1:T(8,128...) fusion(f32[512,12,256]{0,2,1:T(8,128)S(1)} %maximum_multiply_fusion.1,, ...), kind=kLoop, calls=%fused_computation.116 | loop fusion | bytes 67108896 | tf_op jit(solution)/shard_map/dynamic_slice | solution.py:65
  256.4 18.2 %fusion.1 = f32[512,8,256]{0,2,1:T(8,128)} fusion(f32[512,8,256]{0,2,1:T(8,128)} %copy-done.2, s32[]{:T(128)S(6)} %select_n.95, f32[512,8,256]{0,2,1:T(8,128)} %get-tuple-element.16, s32[]{:T(128)S(6)} %select_n.93, f32[512,8,256]{0,2,1:T(8,128)} %get-tuple-element.17, s32[]{:T(128)S(6)} %select_n.91, f32[512,8,256]{0,2,1:T(8,128)} %get-tuple-element.18, ...), kind=kLoop, calls=%fused_computation.37 | loop fusion | flops 19922944 | bytes 41945120 | tf_op jit(solution)/shard_map/add | solution.py:67
  274.6 5.4 %copy.37 = f32[512,8,256]{2,1,0:T(8,128)} copy(f32[512,8,256]{0,2,1:T(8,128)} %fusion.1) | data formatting | bytes 8388608
  (30 shorter events, 0.2 us)
Async XLA Ops:
  7.2 46.0 %all-reduce.5.cloned.1.call-start = ((), (), s32[]{:S(2)}) async-start(), calls=%async_computation | async-start | bytes 917504 | tf_op jit(solution)/shard_map/psum | solution.py:50
  7.2 4.2 %copy-start.6 = (s32[512,14]{0,1:T(8,128)S(1)}, s32[512,14]{0,1:T(8,128)}, u32[]{:S(2)}) copy-start(s32[512,14]{0,1:T(8,128)} %param.23) | copy-start | bytes 86020
  7.2 4.2 %copy-start.13 = (f32[512]{0:T(512)S(1)}, f32[512]{0:T(512)}, u32[]{:S(2)}) copy-start(f32[512]{0:T(512)} %param.26) | copy-start | bytes 6148
  11.4 2.1 copy-start.4
  11.4 2.1 copy-start.14
  17.2 168.3 %all-reduce.7.cloned.1.call-start = ((), (), s32[]{:S(2)}) async-start(), calls=%async_computation.1 | async-start | bytes 917504 | tf_op jit(solution)/shard_map/psum | solution.py:50
  17.3 5.5 %copy-start.17 = (f32[512]{0:T(512)S(1)}, f32[512]{0:T(512)}, u32[]{:S(2)}) copy-start(f32[512]{0:T(512)} %param.27) | copy-start | bytes 6148
  17.3 5.5 %copy-start.18 = (f32[40]{0:T(128)S(1)}, f32[40]{0:T(128)}, u32[]{:S(2)}) copy-start(f32[40]{0:T(128)} %param.29) | copy-start | bytes 484
  17.3 35.8 %copy-start.8 = (f32[40,8,256]{2,1,0:T(8,128)S(1)}, f32[40,8,256]{2,1,0:T(8,128)}, u32[]{:S(2)}) copy-start(f32[40,8,256]{2,1,0:T(8,128)} %param.19) | copy-start | bytes 983044
  17.3 35.8 %copy-start.10 = (f32[12,8,256]{2,1,0:T(8,128)S(1)}, f32[12,8,256]{2,1,0:T(8,128)}, u32[]{:S(2)}) copy-start(f32[12,8,256]{2,1,0:T(8,128)} %param.20) | copy-start | bytes 294916
  17.3 35.8 %copy-start.16 = (s32[40]{0:T(128)S(1)}, s32[40]{0:T(128)}, u32[]{:S(2)}) copy-start(s32[40]{0:T(128)} %param.24) | copy-start | bytes 484
  17.4 35.8 %copy-start.19 = (f32[40]{0:T(128)S(1)}, f32[40]{0:T(128)}, u32[]{:S(2)}) copy-start(f32[40]{0:T(128)} %param.31) | copy-start | bytes 484
  17.4 35.8 %copy-start.20 = (f32[40]{0:T(128)S(1)}, f32[40]{0:T(128)}, u32[]{:S(2)}) copy-start(f32[40]{0:T(128)} %param.30) | copy-start | bytes 484
  17.4 38.0 %copy-start.5 = (f32[14,8,256]{2,1,0:T(8,128)S(1)}, f32[14,8,256]{2,1,0:T(8,128)}, u32[]{:S(2)}) copy-start(f32[14,8,256]{2,1,0:T(8,128)} %param.21) | copy-start | bytes 344068
  17.4 38.0 %copy-start.15 = (f32[14]{0:T(128)S(1)}, f32[14]{0:T(128)}, u32[]{:S(2)}) copy-start(f32[14]{0:T(128)} %param.32) | copy-start | bytes 172
  62.5 2.0 copy-start.1
  64.5 5.0 %copy-start.11 = (s32[8,2]{0,1:T(2,128)S(1)}, s32[8,2]{0,1:T(2,128)}, u32[]{:S(2)}) copy-start(s32[8,2]{0,1:T(2,128)} %param.33) | copy-start | bytes 196
  64.5 47.8 %copy-start.12 = (f32[512]{0:T(512)S(1)}, f32[512]{0:T(512)}, u32[]{:S(2)}) copy-start(f32[512]{0:T(512)} %param.28) | copy-start | bytes 6148
  64.7 45.3 %collective-permute-start = (f32[512,2,256]{0,2,1:T(8,128)S(1)}, f32[512,2,256]{0,2,1:T(8,128)S(1)}, u32[]{:S(2)}, u32[]{:S(2)}) collective-permute-start(f32[512,2,256]{0,2,1:T(8,128)S(1)} %get-tuple-element.33), channel_id=1, source_target_pairs={{0,4},{4,8},{8,12},{12,16},{16,20},{20,24},{24,28},{28,0},{1,5},{5... | collective-permute-start | bytes 3145736 | tf_op jit(solution)/shard_map/ppermute | solution.py:18
  66.2 46.1 %collective-permute-start.1 = (f32[512,2,256]{0,2,1:T(8,128)S(1)}, f32[512,2,256]{0,2,1:T(8,128)}, u32[]{:S(2)}, u32[]{:S(2)}) collective-permute-start(f32[512,2,256]{0,2,1:T(8,128)S(1)} %get-tuple-element.34), channel_id=1, source_target_pairs={{4,0},{8,4},{12,8},{16,12},{20,16},{24,20},{28,24},{0,28},{5,1},{9... | collective-permute-start | bytes 3145736 | tf_op jit(solution)/shard_map/ppermute | solution.py:21
  144.1 7.6 %copy-start = (f32[512,8,256]{0,2,1:T(8,128)}, f32[512,8,256]{0,2,1:T(8,128)S(1)}, u32[]{:S(2)}) copy-start(f32[512,8,256]{0,2,1:T(8,128)S(1)} %fusion) | copy-start | bytes 12582916
  147.7 37.9 %copy-start.3 = (f32[54,8,256]{2,0,1:T(8,128)S(1)}, f32[54,8,256]{2,0,1:T(8,128)}, u32[]{:S(2)}) copy-start(f32[54,8,256]{2,0,1:T(8,128)} %all-reduce.5.cloned.1.call-done) | copy-start | bytes 1327108
  147.7 37.9 %copy-start.9 = (f32[40,8,256]{2,1,0:T(8,128)S(1)}, f32[40,8,256]{2,1,0:T(8,128)}, u32[]{:S(2)}) copy-start(f32[40,8,256]{2,1,0:T(8,128)} %param.19) | copy-start | bytes 983044
  147.7 39.0 %copy-start.7 = (f32[12,8,256]{2,0,1:T(8,128)S(1)}, f32[12,8,256]{2,0,1:T(8,128)}, u32[]{:S(2)}) copy-start(f32[12,8,256]{2,0,1:T(8,128)} %get-tuple-element.52) | copy-start | bytes 294916
  195.5 47.7 %copy-start.2 = (f32[512,8,256]{0,2,1:T(8,128)}, f32[512,8,256]{0,2,1:T(8,128)S(1)}, u32[]{:S(2)}) copy-start(f32[512,8,256]{0,2,1:T(8,128)S(1)} %bitcast_multiply_fusion) | copy-start | bytes 12582916
  195.8 45.3 %collective-permute-start.2 = (f32[512,2,256]{0,2,1:T(8,128)S(1)}, f32[512,2,256]{0,2,1:T(8,128)S(1)}, u32[]{:S(2)}, u32[]{:S(2)}) collective-permute-start(f32[512,2,256]{0,2,1:T(8,128)S(1)} %get-tuple-element.31), channel_id=1, source_target_pairs={{0,4},{4,8},{8,12},{12,16},{16,20},{20,24},{24,28},{28,0},{1,5},{5... | collective-permute-start | bytes 3145736 | tf_op jit(solution)/shard_map/ppermute | solution.py:18
  197.3 46.0 %collective-permute-start.3 = (f32[512,2,256]{0,2,1:T(8,128)S(1)}, f32[512,2,256]{0,2,1:T(8,128)S(1)}, u32[]{:S(2)}, u32[]{:S(2)}) collective-permute-start(f32[512,2,256]{0,2,1:T(8,128)S(1)} %get-tuple-element.32), channel_id=1, source_target_pairs={{4,0},{8,4},{12,8},{16,12},{20,16},{24,20},{28,24},{0,28},{5,1},{9... | collective-permute-start | bytes 3145736 | tf_op jit(solution)/shard_map/ppermute | solution.py:21
Sparse Core Ops, SparseCore 0:
  17.3 35.7 all-reduce.4
  153.0 32.5 all-reduce.6
where the time goes:
time: 288 us; the launch traced here: 287 us
  waiting for transfers between devices  120 us (42%)
  local copies, waits for them, and re-layouts  47.1 us (16%)
  other arithmetic  40.9 us (14%)
  between operations  40 us (14%)
  matrix products  29.2 us (10%)
  starting transfers between devices  9.63 us (3%)
    psum x2, waiting for transfers between devices, pool_update(): sums = lax.psum(local, 'taxa')  63 us
    ppermute x2, waiting for transfers between devices, extended(): lax.ppermute(lax.slice_in_dim(block, block.shape[dim] - width, None, axis...  52.5 us
    add x2, other arithmetic, spread(): return centre - centre * fraction + total / KOFF  34.7 us
    dynamic_slice x2, local copies, waits for them, and re-layouts, spread(): piece = lax.dynamic_slice_in_dim(moved_pad, 2 - offsets[k, 0], rows, 1)  24.5 us
    unnamed x50, local copies, waits for them, and re-layouts  19.6 us
    dot_general x2, matrix products, grow(): gain = jnp.einsum('tm,mrw->trw', mono_w, share, precision=HIGH)  14.2 us
    dot_general x2, matrix products, pool_update(): jnp.dot(prod_w.T, flat, precision=HIGH, preferred_element_type=jnp.float32)  6.51 us
    ppermute x2, starting transfers between devices, extended(): lax.ppermute(lax.slice_in_dim(block, 0, width, axis=dim), axis, backward)  6.5 us
  transfers between devices with their start and end apart: 6, of which 6 were waited for; matrix products, arithmetic and copies ran while one was open for 3% of the time, Pallas kernels for 0%

commit v1 on v0

--- a/solution.py
+++ b/solution.py
@@ -2,11 +2,16 @@
 import jax.numpy as jnp
 from jax import lax
 from jax.sharding import PartitionSpec as P
+from jax.lax import all_gather
 
 KOFF = 8
 DAYS = 2
 HIGH = lax.Precision.HIGHEST
 YIELD = 0.6
+
+
+def carry_signs(my_tile):
+    return all_gather(my_tile, "taxa").sum(axis=0)
 
 
 def extended(block, sides, width):
@@ -47,7 +52,7 @@
     made = jnp.dot(prod_w.T, flat, precision=HIGH, preferred_element_type=jnp.float32)
     need = jnp.dot(upt_w.T, flat, precision=HIGH, preferred_element_type=jnp.float32)
     local = jnp.concatenate([made, need], 0).reshape(-1, rows, width)
-    sums = lax.psum(local, "taxa")
+    sums = carry_signs(local)
     return cell_update(sums, enz, sub, mono, enz_loss, vmax, kmich, khalf, enz_target)
 
 

time: 288 us -> 264 us (0.917)
  waiting for transfers between devices: 120 us -> 98.4 us
  matrix products: 29.2 us -> 24.9 us
    psum x2 -> x0, waiting for transfers between devices: 63 us -> none  [pool_update(): sums = lax.psum(local, 'taxa')]
    all_gather x0 -> x2, waiting for transfers between devices: none -> 37.3 us  [carry_signs(): return all_gather(my_tile, 'taxa').sum(axis=0)]
    ppermute x2, waiting for transfers between devices: 52.5 us -> 56.9 us  [extended(): lax.ppermute(lax.slice_in_dim(block, block.shape[dim] - width, None, axis...]
    reduce_sum x0 -> x2, other arithmetic: none -> 3.28 us  [carry_signs(): return all_gather(my_tile, 'taxa').sum(axis=0)]
    unnamed x50 -> x43, local copies, waits for them, and re-layouts: 19.6 us -> 18.7 us
where the time goes in v1:
time: 264 us; the launch traced here: 263 us
  waiting for transfers between devices  98.4 us (37%)
  local copies, waits for them, and re-layouts  47 us (18%)
  other arithmetic  43.5 us (16%)
  between operations  39.8 us (15%)
  matrix products  24.9 us (9%)
  starting transfers between devices  9.58 us (4%)
    ppermute x2, waiting for transfers between devices, extended(): lax.ppermute(lax.slice_in_dim(block, block.shape[dim] - width, None, axis...  56.9 us
    all_gather x2, waiting for transfers between devices, carry_signs(): return all_gather(my_tile, 'taxa').sum(axis=0)  37.3 us
    add x2, other arithmetic, spread(): return centre - centre * fraction + total / KOFF  34.8 us
    dynamic_slice x2, local copies, waits for them, and re-layouts, spread(): piece = lax.dynamic_slice_in_dim(moved_pad, 2 - offsets[k, 0], rows, 1)  24.5 us
    unnamed x43, local copies, waits for them, and re-layouts  18.7 us
    dot_general x2, matrix products, grow(): gain = jnp.einsum('tm,mrw->trw', mono_w, share, precision=HIGH)  11.4 us
    dot_general x2, matrix products, pool_update(): jnp.dot(prod_w.T, flat, precision=HIGH, preferred_element_type=jnp.float32)  6.5 us
    ppermute x2, starting transfers between devices, extended(): lax.ppermute(lax.slice_in_dim(block, 0, width, axis=dim), axis, backward)  6.5 us
  transfers between devices with their start and end apart: 6, of which 6 were waited for; matrix products, arithmetic and copies ran while one was open for 3% of the time, Pallas kernels for 0%

profile of v1, /device:TPU:0, one launch (start us, length us, event | category | flops | bytes accessed | tf_op | source)
XLA Modules:
  0.0 263.2 jit_solution(14949510732037046983)
XLA Ops:
  7.2 0.0 all-gather.3.cloned.1.call-start
  7.2 0.0 copy-start.4
  7.2 0.0 copy-start.10
  7.2 4.2 %copy.44 = f32[64,8,8,256]{3,1,2,0:T(8,128)S(1)} copy(f32[64,8,8,256]{3,2,1,0:T(8,128)} %bitcast.65) | data formatting | bytes 8388608
  11.4 0.0 copy-start.7
  11.4 0.0 copy-start.11
  11.5 2.5 fusion.48
  14.0 2.1 fusion.56
  16.1 0.1 copy.45
  16.3 0.8 slice_bitcast_fusion.1
  17.1 0.0 all-gather.3.cloned.1.call-update
  17.1 0.0 copy-start.17
  17.1 0.0 copy-start.14
  17.1 0.0 copy-start.5
  17.1 0.0 copy-start.12
  17.1 0.0 copy-start.3
  17.2 0.0 copy-start.15
  17.2 0.0 copy-start.16
  17.2 0.0 all-gather.5.cloned.1.call-start
  17.2 5.3 %copy.34 = f32[512,8,256]{0,2,1:T(8,128)} copy(f32[512,8,256]{2,1,0:T(8,128)} %param.18) | data formatting | bytes 8388608 | tf_op args[0]
  22.6 0.3 fusion.42
  23.0 17.7 %all-gather.3.cloned.1.call-done = f32[4,54,8,256]{3,2,1,0:T(8,128)} async-done(((f32[1,54,8,256]{3,2,1,0:T(8,128)}), f32[4,54,8,256]{3,2,1,0:T(8,128)}) %all-gather.3.cloned.1.call-update) | async-done | bytes 1769488 | tf_op jit(solution)/shard_map/all_gather | solution.py:14
  40.7 1.6 reduce_sum.28
  42.4 0.2 fusion.39
  42.6 0.3 copy_subtract_fusion
  43.0 0.0 copy-done.6
  43.0 0.0 copy-done.13
  43.0 5.7 %bitcast_multiply_fusion.1 = f32[512,8,256]{0,2,1:T(8,128)S(1)} fusion(f32[512,8,256]{0,2,1:T(8,128)} %copy.34, f32[512]{0:T(512)S(1)} %get-tuple-element.58, f32[512]{0:T(512)S(1)} %get-tuple-element.57, f32[14,8,256]{2,1,0:T(8,128)S(1)} %slice.113, f32[14]{0:T(128)S(1)} %copy-done.13, f32[14,8,256]{2,1,0:T(8,128)S(1)} %copy-done.6, ...), kind=kOutput, calls=%fused_computation.71 | convolution fusion | flops 179428352 | bytes 8749112 | tf_op jit(solution)/shard_map/tm,mrw->trw/dot_general | solution.py:60
  48.7 0.0 copy-start.1
  48.7 2.0 copy-done.1
  50.7 1.2 fusion.72
  51.9 1.5 collective-permute-start
  53.3 3.2 %collective-permute-start.1 = (f32[512,2,256]{0,2,1:T(8,128)S(1)}, f32[512,2,256]{0,2,1:T(8,128)}, u32[]{:S(2)}, u32[]{:S(2)}) collective-permute-start(f32[512,2,256]{0,2,1:T(8,128)S(1)} %get-tuple-element.36), channel_id=1, source_target_pairs={{4,0},{8,4},{12,8},{16,12},{20,16},{24,20},{28,24},{0,28},{5,1},{9... | collective-permute-start | bytes 3145736 | tf_op jit(solution)/shard_map/ppermute | solution.py:26
  56.6 0.7 fusion.73
  82.7 16.2 %collective-permute-done = f32[512,2,256]{0,2,1:T(8,128)} collective-permute-done((f32[512,2,256]{0,2,1:T(8,128)}, f32[512,2,256]{0,2,1:T(8,128)}, u32[]{:S(2)}, u32[]{:S(2)}) %collective-permute-start) | collective-permute-done | bytes 1048608 | tf_op jit(solution)/shard_map/ppermute | solution.py:23
  98.9 2.0 collective-permute-done.1
  100.9 3.2 %maximum_multiply_fusion = f32[512,12,256]{0,2,1:T(8,128)S(1)} fusion(f32[512,2,256]{0,2,1:T(8,128)} %collective-permute-done.1, f32[512,8,256]{0,2,1:T(8,128)} %copy-done.1, f32[512,2,256]{0,2,1:T(8,128)} %collective-permute-done, f32[512]{0:T(512)S(1)} %copy-done.9), kind=kLoop, calls=%fused_computation.32 | loop fusion | flops 4718592 | bytes 12584960 | tf_op jit(solution)/shard_map/mul | solution.py:66
  104.1 12.3 %constant_dynamic-slice_fusion.15 = (f32[512,8,256]{0,2,1:T(8,128)}, f32[512,8,256]{0,2,1:T(8,128)}, f32[512,8,256]{0,2,1:T(8,128)}, f32[512,8,256]{0,2,1:T(8,12...) fusion(f32[512,12,256]{0,2,1:T(8,128)S(1)} %maximum_multiply_fusion, ...), kind=kLoop, calls=%fused_computation.133 | loop fusion | bytes 67108896 | tf_op jit(solution)/shard_map/dynamic_slice | solution.py:70
  116.4 16.5 %fusion = f32[512,8,256]{0,2,1:T(8,128)S(1)} fusion(f32[512,8,256]{0,2,1:T(8,128)} %copy-done.1, s32[]{:T(128)S(6)} %select_n.95, f32[512,8,256]{0,2,1:T(8,128)} %get-tuple-element.26, s32[]{:T(128)S(6)} %select_n.93, f32[512,8,256]{0,2,1:T(8,128)} %get-tuple-element.27, s32[]{:T(128)S(6)} %select_n.91, f32[512,8,256]{0,2,1:T(8,128)} %get-tuple-element.28, ...), kind=kLoop, calls=%fused_computation.36 | loop fusion | flops 19922944 | bytes 41945120 | tf_op jit(solution)/shard_map/add | solution.py:72
  132.9 0.0 copy-start
  132.9 4.0 %fusion.47 = f32[40,2048]{1,0:T(8,128)S(1)} fusion(f32[512,2048]{0,1:T(8,128)S(1)} %bitcast.61, s32[512,40]{0,1:T(8,128)S(1)} %copy-done.4, f32[512]{0:T(512)S(1)} %copy-done.10), kind=kOutput, calls=%fused_computation.105 | convolution fusion | flops 503357440 | bytes 4605952 | tf_op jit(solution)/shard_map/dot_general | solution.py:52
  136.9 3.5 %fusion.55 = f32[14,2048]{1,0:T(8,128)S(1)} fusion(f32[512,2048]{0,1:T(8,128)S(1)} %bitcast.62, s32[512,14]{0,1:T(8,128)S(1)} %copy-done.7, f32[512]{0:T(512)S(1)} %copy-done.11), kind=kOutput, calls=%fused_computation.114 | convolution fusion | flops 176175104 | bytes 4339712 | tf_op jit(solution)/shard_map/dot_general | solution.py:53
  140.5 0.1 copy.46
  140.7 0.8 slice_bitcast_fusion
  141.5 0.0 all-gather.5.cloned.1.call-update
  141.5 0.3 fusion.61
  141.8 19.6 %all-gather.5.cloned.1.call-done = f32[4,54,8,256]{3,2,1,0:T(8,128)} async-done(((f32[1,54,8,256]{3,2,1,0:T(8,128)}), f32[4,54,8,256]{3,2,1,0:T(8,128)}) %all-gather.5.cloned.1.call-update) | async-done | bytes 1769488 | tf_op jit(solution)/shard_map/all_gather | solution.py:14
  161.4 1.6 reduce_sum.29
  163.1 0.9 fusion.38
  164.0 0.3 fusion.74
  164.4 0.2 fusion.46
  164.5 5.7 %bitcast_multiply_fusion = f32[512,8,256]{0,2,1:T(8,128)S(1)} fusion(f32[512,8,256]{0,2,1:T(8,128)} %copy-done, f32[512]{0:T(512)S(1)} %get-tuple-element.58, f32[512]{0:T(512)S(1)} %get-tuple-element.57, f32[14,8,256]{2,0,1:T(8,128)S(1)} %get-tuple-element.14, f32[14,8,256]{2,1,0:T(8,128)S(1)} %slice.117, f32[14]{0:T(128)S(1)} %copy-done.13, ...), kind=kOutput, calls=%fused_computation.70 | convolution fusion | flops 179399680 | bytes 8650808 | tf_op jit(solution)/shard_map/tm,mrw->trw/dot_general | solution.py:60
  170.3 0.0 copy-start.2
  170.3 0.2 fusion.71
  170.5 1.5 collective-permute-start.2
  172.0 3.2 %collective-permute-start.3 = (f32[512,2,256]{0,2,1:T(8,128)S(1)}, f32[512,2,256]{0,2,1:T(8,128)S(1)}, u32[]{:S(2)}, u32[]{:S(2)}) collective-permute-start(f32[512,2,256]{0,2,1:T(8,128)S(1)} %get-tuple-element.34), channel_id=1, source_target_pairs={{4,0},{8,4},{12,8},{16,12},{20,16},{24,20},{28,24},{0,28},{5,1},{9... | collective-permute-start | bytes 3145736 | tf_op jit(solution)/shard_map/ppermute | solution.py:26
  175.3 0.7 copy.39
  176.0 0.7 copy.38
  176.7 40.6 %collective-permute-done.2 = f32[512,2,256]{0,2,1:T(8,128)S(1)} collective-permute-done((f32[512,2,256]{0,2,1:T(8,128)S(1)}, f32[512,2,256]{0,2,1:T(8,128)S(1)}, u32[]{:S(2)}, u32[]{:S(2)}) %collective-permute-start.2) | collective-permute-done | bytes 1048608 | tf_op jit(solution)/shard_map/ppermute | solution.py:23
  217.3 2.2 collective-permute-done.3
  219.5 0.8 maximum_multiply_fusion.1
  220.4 12.3 %constant_dynamic-slice_fusion.7 = (f32[512,8,256]{0,2,1:T(8,128)}, f32[512,8,256]{0,2,1:T(8,128)}, f32[512,8,256]{0,2,1:T(8,128)}, f32[512,8,256]{0,2,1:T(8,128...) fusion(f32[512,12,256]{0,2,1:T(8,128)S(1)} %maximum_multiply_fusion.1,, ...), kind=kLoop, calls=%fused_computation.125 | loop fusion | bytes 67108896 | tf_op jit(solution)/shard_map/dynamic_slice | solution.py:70
  232.6 18.2 %fusion.1 = f32[512,8,256]{0,2,1:T(8,128)} fusion(f32[512,8,256]{0,2,1:T(8,128)} %copy-done.2, s32[]{:T(128)S(6)} %select_n.95, f32[512,8,256]{0,2,1:T(8,128)} %get-tuple-element.18, s32[]{:T(128)S(6)} %select_n.93, f32[512,8,256]{0,2,1:T(8,128)} %get-tuple-element.19, s32[]{:T(128)S(6)} %select_n.91, f32[512,8,256]{0,2,1:T(8,128)} %get-tuple-element.20, ...), kind=kLoop, calls=%fused_computation.37 | loop fusion | flops 19922944 | bytes 41945120 | tf_op jit(solution)/shard_map/add | solution.py:72
  250.9 5.4 %copy.37 = f32[512,8,256]{2,1,0:T(8,128)} copy(f32[512,8,256]{0,2,1:T(8,128)} %fusion.1) | data formatting | bytes 8388608
  (26 shorter events, 0.2 us)
Async XLA Ops:
  7.2 33.5 %all-gather.3.cloned.1.call-start = ((), (), s32[]{:S(2)}) async-start(), calls=%async_computation | async-start | bytes 2211840 | tf_op jit(solution)/shard_map/all_gather | solution.py:14
  7.2 4.2 %copy-start.4 = (s32[512,40]{0,1:T(8,128)S(1)}, s32[512,40]{0,1:T(8,128)}, u32[]{:S(2)}) copy-start(s32[512,40]{0,1:T(8,128)} %param.22) | copy-start | bytes 245764
  7.2 4.2 %copy-start.10 = (f32[512]{0:T(512)S(1)}, f32[512]{0:T(512)}, u32[]{:S(2)}) copy-start(f32[512]{0:T(512)} %param.25) | copy-start | bytes 6148
  11.4 2.6 copy-start.7
  11.4 2.6 copy-start.11
  17.1 5.5 %copy-start.17 = (f32[40]{0:T(128)S(1)}, f32[40]{0:T(128)}, u32[]{:S(2)}) copy-start(f32[40]{0:T(128)} %param.29) | copy-start | bytes 484
  17.1 5.5 %copy-start.14 = (f32[512]{0:T(512)S(1)}, f32[512]{0:T(512)}, u32[]{:S(2)}) copy-start(f32[512]{0:T(512)} %param.27) | copy-start | bytes 6148
  17.1 5.5 %copy-start.5 = (f32[12,8,256]{2,1,0:T(8,128)S(1)}, f32[12,8,256]{2,1,0:T(8,128)}, u32[]{:S(2)}) copy-start(f32[12,8,256]{2,1,0:T(8,128)} %param.20) | copy-start | bytes 294916
  17.1 5.5 %copy-start.12 = (s32[40]{0:T(128)S(1)}, s32[40]{0:T(128)}, u32[]{:S(2)}) copy-start(s32[40]{0:T(128)} %param.24) | copy-start | bytes 484
  17.1 25.2 %copy-start.3 = (f32[40,8,256]{2,1,0:T(8,128)S(1)}, f32[40,8,256]{2,1,0:T(8,128)}, u32[]{:S(2)}) copy-start(f32[40,8,256]{2,1,0:T(8,128)} %param.19) | copy-start | bytes 983044
  17.2 25.2 %copy-start.15 = (f32[40]{0:T(128)S(1)}, f32[40]{0:T(128)}, u32[]{:S(2)}) copy-start(f32[40]{0:T(128)} %param.31) | copy-start | bytes 484
  17.2 25.2 %copy-start.16 = (f32[40]{0:T(128)S(1)}, f32[40]{0:T(128)}, u32[]{:S(2)}) copy-start(f32[40]{0:T(128)} %param.30) | copy-start | bytes 484
  17.2 144.3 %all-gather.5.cloned.1.call-start = ((), (), s32[]{:S(2)}) async-start(), calls=%async_computation.1 | async-start | bytes 2211840 | tf_op jit(solution)/shard_map/all_gather | solution.py:14
  22.5 20.4 %copy-start.6 = (f32[14,8,256]{2,1,0:T(8,128)S(1)}, f32[14,8,256]{2,1,0:T(8,128)}, u32[]{:S(2)}) copy-start(f32[14,8,256]{2,1,0:T(8,128)} %param.21) | copy-start | bytes 344068
  22.6 20.4 %copy-start.13 = (f32[14]{0:T(128)S(1)}, f32[14]{0:T(128)}, u32[]{:S(2)}) copy-start(f32[14]{0:T(128)} %param.32) | copy-start | bytes 172
  48.7 2.0 copy-start.1
  50.7 5.9 %copy-start.8 = (s32[8,2]{0,1:T(2,128)S(1)}, s32[8,2]{0,1:T(2,128)}, u32[]{:S(2)}) copy-start(s32[8,2]{0,1:T(2,128)} %param.33) | copy-start | bytes 196
  50.7 50.2 %copy-start.9 = (f32[512]{0:T(512)S(1)}, f32[512]{0:T(512)}, u32[]{:S(2)}) copy-start(f32[512]{0:T(512)} %param.28) | copy-start | bytes 6148
  51.9 47.1 %collective-permute-start = (f32[512,2,256]{0,2,1:T(8,128)}, f32[512,2,256]{0,2,1:T(8,128)}, u32[]{:S(2)}, u32[]{:S(2)}) collective-permute-start(f32[512,2,256]{0,2,1:T(8,128)} %get-tuple-element.35), channel_id=1, source_target_pairs={{0,4},{4,8},{8,12},{12,16},{16,20},{20,24},{24,28},{28,0},{1,5},{5... | collective-permute-start | bytes 3145736 | tf_op jit(solution)/shard_map/ppermute | solution.py:23
  53.3 47.6 %collective-permute-start.1 = (f32[512,2,256]{0,2,1:T(8,128)S(1)}, f32[512,2,256]{0,2,1:T(8,128)}, u32[]{:S(2)}, u32[]{:S(2)}) collective-permute-start(f32[512,2,256]{0,2,1:T(8,128)S(1)} %get-tuple-element.36), channel_id=1, source_target_pairs={{4,0},{8,4},{12,8},{16,12},{20,16},{24,20},{28,24},{0,28},{5,1},{9... | collective-permute-start | bytes 3145736 | tf_op jit(solution)/shard_map/ppermute | solution.py:26
  132.9 7.6 %copy-start = (f32[512,8,256]{0,2,1:T(8,128)}, f32[512,8,256]{0,2,1:T(8,128)S(1)}, u32[]{:S(2)}) copy-start(f32[512,8,256]{0,2,1:T(8,128)S(1)} %fusion) | copy-start | bytes 12582916
  170.3 49.3 %copy-start.2 = (f32[512,8,256]{0,2,1:T(8,128)}, f32[512,8,256]{0,2,1:T(8,128)S(1)}, u32[]{:S(2)}) copy-start(f32[512,8,256]{0,2,1:T(8,128)S(1)} %bitcast_multiply_fusion) | copy-start | bytes 12582916
  170.5 46.8 %collective-permute-start.2 = (f32[512,2,256]{0,2,1:T(8,128)S(1)}, f32[512,2,256]{0,2,1:T(8,128)S(1)}, u32[]{:S(2)}, u32[]{:S(2)}) collective-permute-start(f32[512,2,256]{0,2,1:T(8,128)S(1)} %get-tuple-element.33), channel_id=1, source_target_pairs={{0,4},{4,8},{8,12},{12,16},{16,20},{20,24},{24,28},{28,0},{1,5},{5... | collective-permute-start | bytes 3145736 | tf_op jit(solution)/shard_map/ppermute | solution.py:23
  172.0 47.5 %collective-permute-start.3 = (f32[512,2,256]{0,2,1:T(8,128)S(1)}, f32[512,2,256]{0,2,1:T(8,128)S(1)}, u32[]{:S(2)}, u32[]{:S(2)}) collective-permute-start(f32[512,2,256]{0,2,1:T(8,128)S(1)} %get-tuple-element.34), channel_id=1, source_target_pairs={{4,0},{8,4},{12,8},{16,12},{20,16},{24,20},{28,24},{0,28},{5,1},{9... | collective-permute-start | bytes 3145736 | tf_op jit(solution)/shard_map/ppermute | solution.py:26
Sparse Core Ops, SparseCore 0:
  17.2 23.4 all-gather.2
  141.6 19.7 all-gather.4
